TPU v7x, 512 devices: a whole 4x8x8 slice. The times are simulated.
512 devices in a mesh: tile: 128 (over y, z, core), spec: 4 (over x).
Axes of the slice: x: 4, y: 8, z: 8, core: 2. Of those that a mesh axis runs over, the one named last changes fastest.
Arguments:
- grad_columns: bfloat16 [131072, 512], P('tile', 'spec'), may hold values from -6 to 6
- grad_flux: float32 [16, 131072], P('spec', 'tile'), may hold values from -6 to 6
- remap_part: int32 [131072, 4], P('tile'), may hold values from 0 to 127, all different within a row; in each aligned block of 1024 rows (0 to 1023, 1024 to 2047, ...) at most 64 rows name the same one
- remap_slot: int32 [131072, 4], P('tile'), may hold values from 0 to 1023
- remap_weight: float32 [131072, 4], P('tile'), may hold values from 0.2 to 1
- col_count: int32 [128], P('tile'), may hold values from 341 to 1024, as said below
- neighbors: int32 [131072, 4], P('tile'), may hold values from 0 to 1279, as said below
- kappa: float32 [16], P('spec'), may hold values from 0.03 to 0.2
- thickness: float32 [16, 32], P('spec'), may hold values from 0.2 to 2
- vertical: bfloat16 [16, 32, 32], P('spec'), may hold values from -1 to 1
- reaction: bfloat16 [16, 16], P(None, 'spec'), may hold values from -1.5 to 1.5
Outputs:
- grad_state: bfloat16 [131072, 512], P('tile', 'spec')
- grad_bottom: float32 [16, 131072], P('spec', 'tile')
Inputs may be any that keep to these rules, and one draw needn't show every extreme that they name: `remap_part`: each coarse cell names 4 different partitions; the entries of the cells of one tile (1024 cells) name one partition at most 64 times. `col_count`: live counts of partitions differ up to threefold; one partition holds 1024 live columns and one holds 341. `neighbors`: row p * 1024 + i lists the codes of 4 neighbours of slot i of partition p; every named slot is live; the first partition names no previous and the last no next partition.
All inputs are finite; a program needn't handle non-finite values.
Results may differ from a plain program's by a relative error of at most 0.008.
Values may be sent and summed in bfloat16 or wider, within the bound.
A program may use at most 128 MiB of HBM per device.

v0:
```python
import jax
import jax.numpy as jnp
from jax import lax
from jax.sharding import PartitionSpec as P

SUB = 4


def shifted(block, axis, distance):
    devices = range(lax.axis_size(axis))
    route = [(i - distance, i) for i in devices if i - distance in devices]
    return lax.ppermute(block, axis, route)


def body(
    grad_columns,
    grad_flux,
    remap_part,
    remap_slot,
    remap_weight,
    col_count,
    neighbors,
    kappa,
    thickness,
    vertical,
    reaction,
):
    tiles = lax.axis_size("tile")
    col_max = grad_columns.shape[0]
    rim_width = col_max // 8
    species = kappa.shape[0]
    layers = thickness.shape[1]
    width = species * layers
    cells, per_cell = remap_part.shape
    entries = cells * per_cell
    capacity = 2 * entries // tiles
    nbr_count = neighbors.shape[1]
    dest_flat = remap_part.reshape(-1)
    slot_flat = remap_slot.reshape(-1)
    dest_table = (dest_flat[:, None] == jnp.arange(tiles, dtype=jnp.int32)[None, :]).astype(
        jnp.int32
    )
    earlier = jnp.cumsum(dest_table, axis=0) - dest_table
    rank_within = jnp.sum(earlier * dest_table, axis=1)
    bucket_pos = dest_flat * capacity + rank_within
    entry_values = (remap_weight[:, :, None] * grad_flux.T[:, None, :]).reshape(entries, species)
    send_values = (
        jnp.zeros((tiles * capacity, species), jnp.float32)
        .at[bucket_pos]
        .set(entry_values)
        .reshape(tiles, capacity, species)
    )
    send_slots = (
        jnp.full((tiles * capacity, 1), col_max, jnp.int32)
        .at[bucket_pos]
        .set(slot_flat[:, None])
        .reshape(tiles, capacity, 1)
    )
    recv_values, recv_slots = (
        lax.all_to_all(send_values, "tile", split_axis=0, concat_axis=0, tiled=True),
        lax.all_to_all(send_slots, "tile", split_axis=0, concat_axis=0, tiled=True),
    )
    slot_index = recv_slots.reshape(-1)
    injected = (
        jnp.zeros((col_max + 1, species), jnp.float32)
        .at[slot_index]
        .add(recv_values.reshape(-1, species))[:col_max]
    )
    live_mask = (jnp.arange(col_max) < col_count[0]).astype(jnp.float32)[:, None]
    adjoint = live_mask * (
        grad_columns.astype(jnp.float32)
        + (injected[:, :, None] * thickness[None, :, :]).reshape(col_max, width)
    )
    rate_row = jnp.repeat(kappa, layers)[None, :]
    eye_block = jnp.eye(species, dtype=jnp.bfloat16)
    block_operator = jnp.einsum("slm,st->sltm", vertical, eye_block).reshape(width, width)
    target_rows = jnp.arange(col_max + 2 * rim_width, dtype=jnp.int32)[:, None]
    count_matrix = jnp.zeros((col_max + 2 * rim_width, col_max), jnp.float32)
    for column in range(nbr_count):
        count_matrix = count_matrix + (neighbors[:, column][None, :] == target_rows).astype(
            jnp.float32
        )
    zero_rest = jnp.zeros((col_max - 2 * rim_width, width), jnp.float32)
    for substep in range(SUB):
        spread = rate_row * adjoint
        extended = jnp.dot(
            count_matrix,
            spread,
            precision=lax.Precision.HIGHEST,
            preferred_element_type=jnp.float32,
        )
        to_previous = extended[col_max : col_max + rim_width]
        to_following = extended[col_max + rim_width :]
        from_following = shifted(to_previous.astype(jnp.bfloat16), "tile", -1).astype(
            to_previous.dtype
        )
        from_previous = shifted(to_following.astype(jnp.bfloat16), "tile", 1).astype(
            to_following.dtype
        )
        rim_terms = jnp.concatenate([from_previous, from_following, zero_rest], axis=0)
        bedload = adjoint - nbr_count * rate_row * adjoint + extended[:col_max] + rim_terms
        adjoint = jnp.dot(
            bedload.astype(jnp.bfloat16), block_operator, preferred_element_type=jnp.float32
        )
    rounded = adjoint.astype(jnp.bfloat16)
    piece = lax.all_gather(rounded, "spec", axis=1, tiled=True)
    piece_species = piece.shape[1] // layers
    mixed = jnp.einsum(
        "jsl,st->jtl",
        piece.reshape(col_max, piece_species, layers),
        reaction,
        preferred_element_type=jnp.float32,
    )
    grad_state = mixed.reshape(col_max, width).astype(jnp.bfloat16)
    top_layer = mixed[:, :, 0]
    padded_top = jnp.concatenate([top_layer, jnp.zeros((1, species), jnp.float32)], axis=0)
    answer = padded_top[slot_index].reshape(tiles, capacity, species)
    returned = lax.all_to_all(
        answer.astype(jnp.bfloat16), "tile", split_axis=0, concat_axis=0, tiled=True
    ).astype(answer.dtype)
    picked = returned.reshape(-1, species)[bucket_pos]
    grad_bottom = jnp.sum(
        picked.reshape(cells, per_cell, species) * remap_weight[:, :, None], axis=1
    ).T
    return (grad_state, grad_bottom)


def solution(mesh):
    placed = (
        P("tile", "spec"),
        P("spec", "tile"),
        P("tile", None),
        P("tile", None),
        P("tile", None),
        P("tile"),
        P("tile", None),
        P("spec"),
        P("spec", None),
        P("spec", None, None),
        P(None, "spec"),
    )
    return jax.shard_map(
        body,
        mesh=mesh,
        in_specs=placed,
        out_specs=(P("tile", "spec"), P("spec", "tile")),
        check_vma=False,
    )
```

profile of v0, /device:TPU:1, one launch (start us, length us, event | category | flops | bytes accessed | tf_op | source)
XLA Modules:
  0.0 333.4 jit_solution(15578686047485542764)
XLA Ops:
  15.0 15.5 %scatter_custom_fusion = s32[8192]{0:T(1024)S(1)} fusion(s32[4096]{0:T(1024)S(1)} %bitcast.68, s32[4096]{0:T(1024)S(1)} %reshape.172, s32[]{:T(128)} %constant.8.clone.1), kind=kCustom, calls=%fused_computation.84 | custom fusion | bytes 32772 | tf_op jit(solution)/shard_map/scatter | solution.py:56
  31.2 19.0 %all-to-all-start = ((s32[128,64,1]{1,2,0:T(1,128)}), s32[128,64,1]{1,2,0:T(1,128)S(1)}, u32[]{:S(2)}, u32[]{:S(2)}) async-start(s32[128,64,1]{1,2,0:T(1,128)} %bitcast.6), calls=%async_computation | async-start | bytes 131072 | tf_op jit(solution)/shard_map/all_to_all | solution.py:61
  54.7 12.8 %scatter_custom_fusion.1 = f32[8192,4]{1,0:T(8,128)} fusion(s32[4096]{0:T(1024)S(1)} %bitcast.69, f32[4096,4]{1,0:T(8,128)S(1)} %copy.105, f32[]{:T(128)} %constant.7.clone.1), kind=kCustom, calls=%fused_computation.34 | custom fusion | bytes 131076 | tf_op jit(solution)/shard_map/scatter | solution.py:50
  67.5 3.0 copy.107
  71.5 13.7 %all-to-all-start.1 = ((f32[128,1,256]{2,1,0:T(1,128)}), f32[128,1,256]{2,1,0:T(1,128)S(1)}, u32[]{:S(2)}, u32[]{:S(2)}) async-start(f32[128,1,256]{2,1,0:T(1,128)} %reshape.210), calls=%async_computation.1 | async-start | bytes 262144 | tf_op jit(solution)/shard_map/all_to_all | solution.py:60
  86.8 10.7 %all-to-all-done.1 = f32[128,1,256]{2,1,0:T(1,128)S(1)} async-done(((f32[128,1,256]{2,1,0:T(1,128)}), f32[128,1,256]{2,1,0:T(1,128)S(1)}, u32[]{:S(2)}, u32[]{:S(2)}) %all-to-all-start.1) | async-done | bytes 131104 | tf_op jit(solution)/shard_map/all_to_all | solution.py:60
  99.2 2.7 copy.125
  101.9 44.8 %scatter_custom_fusion.2 = f32[1025,4]{1,0:T(8,128)S(1)} fusion(s32[8192]{0:T(1024)S(1)} %bitcast.65, f32[8192,4]{1,0:T(8,128)} %bitcast.56, f32[]{:T(128)} %constant.7.clone.1), kind=kCustom, calls=%fused_computation.66 | custom fusion | flops 32768 | bytes 16912 | tf_op jit(solution)/shard_map/scatter-add | solution.py:67
  147.2 6.5 %fusion.73 = (bf16[1280,128]{1,0:T(8,128)(2,1)S(1)}, f32[1280,128]{1,0:T(8,128)S(1)}) fusion(f32[1024,128]{1,0:T(8,128)S(1)} %copy.111, bf16[1024,128]{1,0:T(8,128)(2,1)S(1)} %copy-done.1, f32[128]{0:T(128)S(1)} %broadcast_in_dim_reshape.8, f32[128]{0:T(128)S(1)} %mul.146, f32[1024]{0:T(1024)S(1)} %fusion.61, s32[1024]{0:T(1024)S(1)} %bitcast.80, ...), kind=kOutput, calls=%fused_computation.103 | convolution fusion | flops 2028503040 | bytes 1790976 | tf_op jit(solution)/shard_map/dot_general | solution.py:86
  153.7 3.0 collective-permute-start
  156.7 5.6 %collective-permute-start.1 = (bf16[128,128]{1,0:T(8,128)(2,1)S(1)}, bf16[128,128]{1,0:T(8,128)(2,1)S(1)}, u32[]{:S(2)}, u32[]{:S(2)}) collective-permute-start(bf16[128,128]{1,0:T(8,128)(2,1)S(1)} %get-tuple-element.19), channel_id=1, source_target_pairs={{4,0},{8,4},{12,8},{16,12},{20,16},{24,20},{28,24},{32,28},{36,32}... | collective-permute-start | bytes 98312 | tf_op jit(solution)/shard_map/ppermute | solution.py:12
  163.4 6.3 %fusion.74 = (bf16[1280,128]{1,0:T(8,128)(2,1)S(1)}, f32[1280,128]{1,0:T(8,128)S(1)}) fusion(f32[1024,128]{1,0:T(8,128)S(1)} %fusion.57, f32[128]{0:T(128)S(1)} %broadcast_in_dim_reshape.8, s32[1024]{0:T(1024)S(1)} %bitcast.81, s32[1024]{0:T(1024)S(1)} %bitcast.85, s32[1024]{0:T(1024)S(1)} %bitcast.77, s32[1024]{0:T(1024)S(1)} %bitcast.73), kind=kOutput, calls=%fused_computation.104 | convolution fusion | flops 2027978752 | bytes 1524224 | tf_op jit(solution)/shard_map/dot_general | solution.py:86
  174.3 5.8 %collective-permute-done.3 = bf16[128,128]{1,0:T(8,128)(2,1)S(1)} collective-permute-done((bf16[128,128]{1,0:T(8,128)(2,1)S(1)}, bf16[128,128]{1,0:T(8,128)(2,1)S(1)}, u32[]{:S(2)}, u32[]{:S(2)}) %collective-permute-start.3) | collective-permute-done | bytes 32800 | tf_op jit(solution)/shard_map/ppermute | solution.py:12
  180.4 6.3 %fusion.75 = (bf16[1280,128]{1,0:T(8,128)(2,1)S(1)}, f32[1280,128]{1,0:T(8,128)S(1)}) fusion(f32[1024,128]{1,0:T(8,128)S(1)} %fusion.55, f32[128]{0:T(128)S(1)} %broadcast_in_dim_reshape.8, s32[1024]{0:T(1024)S(1)} %bitcast.82, s32[1024]{0:T(1024)S(1)} %bitcast.86, s32[1024]{0:T(1024)S(1)} %bitcast.78, s32[1024]{0:T(1024)S(1)} %bitcast.74), kind=kOutput, calls=%fused_computation.105 | convolution fusion | flops 2027978752 | bytes 1524224 | tf_op jit(solution)/shard_map/dot_general | solution.py:86
  188.7 2.9 collective-permute-start.5
  194.3 6.3 %fusion.76 = (bf16[1280,128]{1,0:T(8,128)(2,1)S(1)}, f32[1280,128]{1,0:T(8,128)S(1)}) fusion(f32[1024,128]{1,0:T(8,128)S(1)} %fusion.53, f32[128]{0:T(128)S(1)} %broadcast_in_dim_reshape.8, s32[1024]{0:T(1024)S(1)} %bitcast.83, s32[1024]{0:T(1024)S(1)} %bitcast.87, s32[1024]{0:T(1024)S(1)} %bitcast.79, s32[1024]{0:T(1024)S(1)} %bitcast.75), kind=kOutput, calls=%fused_computation.106 | convolution fusion | flops 2027978752 | bytes 1524224 | tf_op jit(solution)/shard_map/dot_general | solution.py:86
  204.9 2.8 collective-permute-done.7
  208.8 37.7 %all-gather.2.cloned.1.call-done = bf16[1024,512]{1,0:T(8,128)(2,1)} async-done(((bf16[1024,128]{1,0:T(8,128)(2,1)}), bf16[1024,512]{1,0:T(8,128)(2,1)}) %all-gather.2.cloned.1.call-update) | async-done | bytes 1048592 | tf_op jit(solution)/shard_map/all_gather | solution.py:106
  249.0 24.0 %gather_fusion = bf16[8192,4]{1,0:T(8,128)(2,1)S(1)} fusion(bf16[1025,4]{1,0:T(8,128)(2,1)S(1)} %concatenate.19.clone, s32[8192]{0:T(1024)S(1)} %broadcast_clamp_fusion), kind=kCustom, calls=%fused_computation | custom fusion | bytes 163840 | tf_op jit(solution)/shard_map/gather | solution.py:117
  274.9 16.2 %all-to-all-start.2 = ((bf16[128,2,128]{2,1,0:T(2,128)(2,1)}), bf16[128,2,128]{2,1,0:T(2,128)(2,1)S(1)}, u32[]{:S(2)}, u32[]{:S(2)}) async-start(bf16[128,2,128]{2,1,0:T(2,128)(2,1)} %reshape.212), calls=%async_computation.2 | async-start | bytes 131072 | tf_op jit(solution)/shard_map/all_to_all | solution.py:118
  292.0 10.5 %all-to-all-done.2 = bf16[128,2,128]{2,1,0:T(2,128)(2,1)S(1)} async-done(((bf16[128,2,128]{2,1,0:T(2,128)(2,1)}), bf16[128,2,128]{2,1,0:T(2,128)(2,1)S(1)}, u32[]{:S(2)}, u32[]{:S(2)}) %all-to-all-start.2) | async-done | bytes 65568 | tf_op jit(solution)/shard_map/all_to_all | solution.py:118
  302.7 4.3 %copy.126 = f32[128,64,4]{2,1,0:T(8,128)} copy(bf16[128,64,4]{0,1,2:T(8,128)(2,1)S(1)} %copy.117) | data formatting | bytes 196608 | tf_op jit(solution)/shard_map/reshape | solution.py:121
  307.0 13.0 %gather_fusion.1 = f32[4096,4]{1,0:T(8,128)S(1)} fusion(f32[8192,4]{1,0:T(8,128)} %bitcast.52, s32[4096]{0:T(1024)S(1)} %broadcast_clamp_fusion.1), kind=kCustom, calls=%fused_computation.1 | custom fusion | bytes 147456 | tf_op jit(solution)/shard_map/gather | solution.py:121
  320.0 5.6 %multiply_reduce_fusion = f32[1024,4]{1,0:T(8,128)S(1)} fusion(f32[1024,4,4]{2,1,0:T(4,128)S(1)} %bitcast.55, f32[1024,4]{1,0:T(8,128)S(1)} %copy.104), kind=kLoop, calls=%fused_computation.33 | loop fusion | flops 28672 | bytes 98304 | tf_op jit(solution)/shard_map/reduce_sum | solution.py:122
  (107 shorter events, 38.8 us)
Async XLA Ops:
  7.2 240.9 %copy-start = (bf16[16,4]{0,1:T(4,128)(2,1)S(1)}, bf16[16,4]{0,1:T(4,128)(2,1)}, u32[]{:S(2)}) copy-start(bf16[16,4]{0,1:T(4,128)(2,1)} %param.21) | copy-start | bytes 388
  12.2 38.7 %copy-start.6 = (f32[4,32]{1,0:T(4,128)S(1)}, f32[4,32]{1,0:T(4,128)}, u32[]{:S(2)}) copy-start(f32[4,32]{1,0:T(4,128)} %param.19) | copy-start | bytes 1540
  12.2 38.8 %copy-start.7 = (f32[4]{0:T(128)S(1)}, f32[4]{0:T(128)}, u32[]{:S(2)}) copy-start(f32[4]{0:T(128)} %param.18) | copy-start | bytes 52
  12.2 38.9 %copy-start.5 = (s32[1024,4]{0,1:T(4,128)S(1)}, s32[1024,4]{0,1:T(4,128)}, u32[]{:S(2)}) copy-start(s32[1024,4]{0,1:T(4,128)} %param.17) | copy-start | bytes 49156
  12.2 39.0 %copy-start.4 = (f32[1024,4]{0,1:T(4,128)S(1)}, f32[1024,4]{0,1:T(4,128)}, u32[]{:S(2)}) copy-start(f32[1024,4]{0,1:T(4,128)} %param.15) | copy-start | bytes 49156
  12.2 39.5 %copy-start.3 = (f32[4,1024]{1,0:T(4,128)S(1)}, f32[4,1024]{1,0:T(4,128)}, u32[]{:S(2)}) copy-start(f32[4,1024]{1,0:T(4,128)} %param.12) | copy-start | bytes 49156
  31.2 40.3 %all-to-all-start = ((s32[128,64,1]{1,2,0:T(1,128)}), s32[128,64,1]{1,2,0:T(1,128)S(1)}, u32[]{:S(2)}, u32[]{:S(2)}) async-start(s32[128,64,1]{1,2,0:T(1,128)} %bitcast.6), calls=%async_computation | async-start | bytes 131072 | tf_op jit(solution)/shard_map/all_to_all | solution.py:61
  54.7 16.7 %copy-start.2 = (bf16[4,32,32]{2,1,0:T(8,128)(2,1)S(1)}, bf16[4,32,32]{2,1,0:T(8,128)(2,1)}, u32[]{:S(2)}) copy-start(bf16[4,32,32]{2,1,0:T(8,128)(2,1)} %param.20) | copy-start | bytes 24580
  71.5 26.0 %all-to-all-start.1 = ((f32[128,1,256]{2,1,0:T(1,128)}), f32[128,1,256]{2,1,0:T(1,128)S(1)}, u32[]{:S(2)}, u32[]{:S(2)}) async-start(f32[128,1,256]{2,1,0:T(1,128)} %reshape.210), calls=%async_computation.1 | async-start | bytes 262144 | tf_op jit(solution)/shard_map/all_to_all | solution.py:60
  85.3 161.3 %all-gather.2.cloned.1.call-start = ((), (), s32[]{:S(2)}) async-start(), calls=%async_computation.3 | async-start | bytes 1310720 | tf_op jit(solution)/shard_map/all_gather | solution.py:106
  99.0 48.2 %copy-start.1 = (bf16[1024,128]{1,0:T(8,128)(2,1)S(1)}, bf16[1024,128]{1,0:T(8,128)(2,1)}, u32[]{:S(2)}) copy-start(bf16[1024,128]{1,0:T(8,128)(2,1)} %param.11) | copy-start | bytes 786436
  153.7 8.8 %collective-permute-start = (bf16[128,128]{1,0:T(8,128)(2,1)S(1)}, bf16[128,128]{1,0:T(8,128)(2,1)S(1)}, u32[]{:S(2)}, u32[]{:S(2)}) collective-permute-start(bf16[128,128]{1,0:T(8,128)(2,1)S(1)} %get-tuple-element.18), channel_id=1, source_target_pairs={{0,4},{4,8},{8,12},{12,16},{16,20},{20,24},{24,28},{28,32},{32,36}... | collective-permute-start | bytes 98312 | tf_op jit(solution)/shard_map/ppermute | solution.py:12
  156.7 6.2 %collective-permute-start.1 = (bf16[128,128]{1,0:T(8,128)(2,1)S(1)}, bf16[128,128]{1,0:T(8,128)(2,1)S(1)}, u32[]{:S(2)}, u32[]{:S(2)}) collective-permute-start(bf16[128,128]{1,0:T(8,128)(2,1)S(1)} %get-tuple-element.19), channel_id=1, source_target_pairs={{4,0},{8,4},{12,8},{16,12},{20,16},{24,20},{28,24},{32,28},{36,32}... | collective-permute-start | bytes 98312 | tf_op jit(solution)/shard_map/ppermute | solution.py:12
  169.7 4.6 %collective-permute-start.2 = (bf16[128,128]{1,0:T(8,128)(2,1)S(1)}, bf16[128,128]{1,0:T(8,128)(2,1)S(1)}, u32[]{:S(2)}, u32[]{:S(2)}) collective-permute-start(bf16[128,128]{1,0:T(8,128)(2,1)S(1)} %get-tuple-element.16), channel_id=1, source_target_pairs={{0,4},{4,8},{8,12},{12,16},{16,20},{20,24},{24,28},{28,32},{32,36}... | collective-permute-start | bytes 98312 | tf_op jit(solution)/shard_map/ppermute | solution.py:12
  171.6 8.5 %collective-permute-start.3 = (bf16[128,128]{1,0:T(8,128)(2,1)S(1)}, bf16[128,128]{1,0:T(8,128)(2,1)S(1)}, u32[]{:S(2)}, u32[]{:S(2)}) collective-permute-start(bf16[128,128]{1,0:T(8,128)(2,1)S(1)} %get-tuple-element.17), channel_id=1, source_target_pairs={{4,0},{8,4},{12,8},{16,12},{20,16},{24,20},{28,24},{32,28},{36,32}... | collective-permute-start | bytes 98312 | tf_op jit(solution)/shard_map/ppermute | solution.py:12
  186.8 4.8 %collective-permute-start.4 = (bf16[128,128]{1,0:T(8,128)(2,1)S(1)}, bf16[128,128]{1,0:T(8,128)(2,1)S(1)}, u32[]{:S(2)}, u32[]{:S(2)}) collective-permute-start(bf16[128,128]{1,0:T(8,128)(2,1)S(1)} %get-tuple-element.14), channel_id=1, source_target_pairs={{0,4},{4,8},{8,12},{12,16},{16,20},{20,24},{24,28},{28,32},{32,36}... | collective-permute-start | bytes 98312 | tf_op jit(solution)/shard_map/ppermute | solution.py:12
  188.7 5.2 %collective-permute-start.5 = (bf16[128,128]{1,0:T(8,128)(2,1)S(1)}, bf16[128,128]{1,0:T(8,128)(2,1)S(1)}, u32[]{:S(2)}, u32[]{:S(2)}) collective-permute-start(bf16[128,128]{1,0:T(8,128)(2,1)S(1)} %get-tuple-element.15), channel_id=1, source_target_pairs={{4,0},{8,4},{12,8},{16,12},{20,16},{24,20},{28,24},{32,28},{36,32}... | collective-permute-start | bytes 98312 | tf_op jit(solution)/shard_map/ppermute | solution.py:12
  200.6 4.3 %collective-permute-start.6 = (bf16[128,128]{1,0:T(8,128)(2,1)S(1)}, bf16[128,128]{1,0:T(8,128)(2,1)S(1)}, u32[]{:S(2)}, u32[]{:S(2)}) collective-permute-start(bf16[128,128]{1,0:T(8,128)(2,1)S(1)} %get-tuple-element.12), channel_id=1, source_target_pairs={{0,4},{4,8},{8,12},{12,16},{16,20},{20,24},{24,28},{28,32},{32,36}... | collective-permute-start | bytes 98312 | tf_op jit(solution)/shard_map/ppermute | solution.py:12
  202.5 5.2 %collective-permute-start.7 = (bf16[128,128]{1,0:T(8,128)(2,1)S(1)}, bf16[128,128]{1,0:T(8,128)(2,1)S(1)}, u32[]{:S(2)}, u32[]{:S(2)}) collective-permute-start(bf16[128,128]{1,0:T(8,128)(2,1)S(1)} %get-tuple-element.13), channel_id=1, source_target_pairs={{4,0},{8,4},{12,8},{16,12},{20,16},{24,20},{28,24},{32,28},{36,32}... | collective-permute-start | bytes 98312 | tf_op jit(solution)/shard_map/ppermute | solution.py:12
  274.9 27.6 %all-to-all-start.2 = ((bf16[128,2,128]{2,1,0:T(2,128)(2,1)}), bf16[128,2,128]{2,1,0:T(2,128)(2,1)S(1)}, u32[]{:S(2)}, u32[]{:S(2)}) async-start(bf16[128,2,128]{2,1,0:T(2,128)(2,1)} %reshape.212), calls=%async_computation.2 | async-start | bytes 131072 | tf_op jit(solution)/shard_map/all_to_all | solution.py:118
Sparse Core Ops, SparseCore 0:
  208.9 37.5 all-gather.1
where the time goes:
time: 339 us; the launch traced here: 333 us
  local copies, waits for them, and re-layouts  92.6 us (27%)
  starting transfers between devices  71.2 us (21%)
  waiting for transfers between devices  70.3 us (21%)
  other arithmetic  55.5 us (16%)
  matrix products  28.2 us (8%)
  between operations  15.5 us (5%)
    scatter-add x1, other arithmetic, body(): injected = jnp.zeros((col_max + 1, species), jnp.float32).at[slot_index]....  44.8 us
    all_gather x1, waiting for transfers between devices, body(): piece = lax.all_gather(rounded, 'spec', axis=1, tiled=True)  37.7 us
    dot_general x4, matrix products, body(): jnp.dot(count_matrix, spread, precision=lax.Precision.HIGHEST, preferred_...  25.4 us
    gather x1, local copies, waits for them, and re-layouts, body(): answer = padded_top[slot_index].reshape(tiles, capacity, species)  24 us
    ppermute x8, starting transfers between devices, shifted(): return lax.ppermute(block, axis, route)  22.3 us
    all_to_all x1, starting transfers between devices, body(): lax.all_to_all(send_slots, 'tile', split_axis=0, concat_axis=0, tiled=True)  19 us
    all_to_all x1, starting transfers between devices, body(): lax.all_to_all(answer.astype(jnp.bfloat16), 'tile', split_axis=0, concat_...  16.2 us
    scatter x1, local copies, waits for them, and re-layouts, body(): send_slots = jnp.full((tiles * capacity, 1), col_max, jnp.int32).at[bucke...  15.5 us
  transfers between devices with their start and end apart: 12, of which 7 were waited for; matrix products, arithmetic and copies ran while one was open for 7% of the time, Pallas kernels for 0%

commit v1 on v0

v1 whole, which is shorter than its diff:
```python
import functools

import jax
import jax.numpy as jnp
from jax import lax
from jax.experimental import pallas as pl
from jax.experimental.pallas import tpu as pltpu
from jax.sharding import PartitionSpec as P

SUB = 4
F32 = jnp.float32
BF16 = jnp.bfloat16
MESH = pl.DeviceIdType.MESH
HIGH = lax.Precision.HIGHEST
NT = (((1,), (1,)), ((), ()))
RADIX = 32
PLANES = 6


def dot(a, b):
    return jnp.dot(a, b, preferred_element_type=F32)


def iota(shape, dim):
    return lax.broadcasted_iota(jnp.int32, shape, dim)


def onehot(condition):
    return jnp.where(condition, 1.0, 0.0).astype(BF16)


def dispatch_kernel(tiles, capacity, part_ref, slot_ref, weight_ref, flux_ref, send_ref, rank_ref):
    per_cell, cells = part_ref.shape
    species = flux_ref.shape[0]
    chunk = 256
    before = onehot(iota((chunk, chunk), 0) < iota((chunk, chunk), 1))
    carry = jnp.zeros((tiles, 1), F32)
    total = jnp.zeros((tiles, PLANES * capacity), F32)
    for r in range(per_cell):
        hit = part_ref[r : r + 1, :] == iota((tiles, cells), 0)
        owner = jnp.where(hit, 1.0, 0.0)
        owner_b = owner.astype(BF16)
        for k in range(0, cells, chunk):
            piece = owner[:, k : k + chunk]
            earlier = dot(owner_b[:, k : k + chunk], before) + carry
            rank_ref[r : r + 1, k : k + chunk] = jnp.sum(piece * earlier, axis=0, keepdims=True)
            carry = carry + jnp.sum(piece, axis=1, keepdims=True)
        place = rank_ref[r : r + 1, :].astype(jnp.int32) == iota((capacity, cells), 0)
        slot = slot_ref[r : r + 1, :]
        weight = weight_ref[r : r + 1, :]
        rows = [weight * flux_ref[s : s + 1, :] for s in range(species)]
        rows.append((slot // RADIX).astype(F32))
        rows.append((slot % RADIX).astype(F32))
        wide = jnp.concatenate([jnp.where(place, row, 0.0).astype(BF16) for row in rows], axis=0)
        total = total + lax.dot_general(owner_b, wide, NT, preferred_element_type=F32)
    send_ref[...] = total.astype(BF16)


def column_kernel(
    tiles,
    groups,
    recv_ref,
    columns_ref,
    count_ref,
    neighbors_ref,
    kappa_ref,
    thickness_ref,
    vertical_ref,
    reaction_ref,
    state_ref,
    answer_ref,
    names,
    adjoint,
    operator,
    mixer,
    halo_out,
    halo_in,
    gathered,
    halo_send,
    halo_recv,
    gather_send,
    gather_recv,
):
    slots, width = columns_ref.shape
    species, layers = thickness_ref.shape
    rim = slots // 8
    nbr_count = neighbors_ref.shape[0]
    entries = recv_ref.shape[1]
    tile, spec = lax.axis_index("tile"), lax.axis_index("spec")
    following = lax.rem(tile + 1, tiles)
    previous = lax.rem(tile + tiles - 1, tiles)
    peers = [lax.rem(spec + d, groups) for d in range(1, groups)]

    barrier = pltpu.get_barrier_semaphore()
    for other in (previous, following):
        pl.semaphore_signal(barrier, inc=1, device_id=(other, spec), device_id_type=MESH)
    for other in peers:
        pl.semaphore_signal(barrier, inc=1, device_id=(tile, other), device_id_type=MESH)

    step = 256
    for m in range(0, slots + 2 * rim, step):
        code = iota((step, slots), 0) + m
        count = jnp.zeros((step, slots), F32)
        for n in range(nbr_count):
            count = count + jnp.where(neighbors_ref[n : n + 1, :] == code, 1.0, 0.0)
        names[m : m + step, :] = count.astype(BF16)

    lane = iota((1, width), 1)
    layer_to_lane = onehot(iota((layers, width), 0) == iota((layers, width), 1) % layers)
    same_species = iota((width, width), 0) // layers == iota((width, width), 1) // layers
    operator[...] = jnp.where(same_species, dot(vertical_ref[...], layer_to_lane), 0.0).astype(BF16)
    all_species = groups * species
    wide = groups * width
    row_species = onehot(iota((wide, all_species), 0) // layers == iota((wide, all_species), 1))
    lane_species = onehot(iota((species, width), 0) == iota((species, width), 1) // layers)
    by_row = dot(row_species, reaction_ref[...]).astype(BF16)
    spread_out = dot(by_row, lane_species)
    same_layer = iota((wide, width), 0) % layers == iota((wide, width), 1) % layers
    mixer[...] = jnp.where(same_layer, spread_out, 0.0).astype(BF16)
    rate = jnp.zeros((1, width), F32)
    for s in range(species):
        rate = rate + jnp.where(lane // layers == s, kappa_ref[0:1, s : s + 1], 0.0)
    thick_rows = jnp.dot(
        thickness_ref[...], layer_to_lane.astype(F32), precision=HIGH, preferred_element_type=F32
    )
    thick = jnp.zeros((1, width), F32)
    for s in range(species):
        thick = thick + jnp.where(lane // layers == s, thick_rows[s : s + 1, :], 0.0)

    block = 1024
    digits = slots // RADIX
    injected = jnp.zeros((digits, species * RADIX), F32)
    for e in range(0, entries, block):
        high = recv_ref[species : species + 1, e : e + block].astype(jnp.int32)
        low = recv_ref[species + 1 : species + 2, e : e + block].astype(jnp.int32)
        high_hot = onehot(high == iota((digits, block), 0))
        low_hit = low == iota((RADIX, block), 0)
        values = [
            jnp.where(low_hit, recv_ref[s : s + 1, e : e + block], 0.0).astype(BF16)
            for s in range(species)
        ]
        injected = injected + lax.dot_general(
            high_hot, jnp.concatenate(values, axis=0), NT, preferred_element_type=F32
        )
    slot_digit = onehot(iota((slots, digits), 0) // RADIX == iota((slots, digits), 1))
    own_low = iota((slots, width), 0) % RADIX == iota((slots, width), 1) % RADIX
    block_ones = onehot(same_species)
    upper = injected.astype(BF16)
    lower = (injected - upper.astype(F32)).astype(BF16)
    added = jnp.zeros((slots, width), F32)
    for part in (upper, lower):
        chosen = jnp.where(own_low, dot(slot_digit, part), 0.0).astype(BF16)
        added = added + dot(chosen, block_ones)
    live = iota((slots, 1), 0) < count_ref[0, 0]
    adjoint[...] = jnp.where(live, columns_ref[...].astype(F32) + thick * added, 0.0)

    pl.semaphore_wait(barrier, groups + 1)

    keep = 1.0 - nbr_count * rate
    for substep in range(SUB):
        spread = (rate * adjoint[...]).astype(BF16)
        outer = dot(names[slots : slots + 2 * rim, :], spread)
        halo_out[substep] = outer.astype(BF16)
        copies = []
        for side, other in enumerate((previous, following)):
            copy = pltpu.make_async_remote_copy(
                src_ref=halo_out.at[substep, pl.ds(side * rim, rim)],
                dst_ref=halo_in.at[substep, pl.ds((1 - side) * rim, rim)],
                send_sem=halo_send.at[substep, side],
                recv_sem=halo_recv.at[substep, side],
                device_id=(other, spec),
                device_id_type=MESH,
            )
            copy.start()
            copies.append(copy)
        inner = dot(names[0:slots, :], spread)
        bedload = keep * adjoint[...] + inner
        rest = bedload[2 * rim :, :].astype(BF16)
        rest = dot(rest, operator[...])
        for copy in copies:
            copy.wait()
        front = bedload[: 2 * rim, :] + halo_in[substep].astype(F32)
        front = dot(front.astype(BF16), operator[...])
        if substep < SUB - 1:
            adjoint[0 : 2 * rim, :] = front
            adjoint[2 * rim :, :] = rest
        else:
            gathered[spec, 0 : 2 * rim, :] = front.astype(BF16)
            gathered[spec, 2 * rim :, :] = rest.astype(BF16)

    copies = []
    for d, other in enumerate(peers):
        copy = pltpu.make_async_remote_copy(
            src_ref=gathered.at[spec],
            dst_ref=gathered.at[spec],
            send_sem=gather_send.at[d],
            recv_sem=gather_recv.at[d],
            device_id=(tile, other),
            device_id_type=MESH,
        )
        copy.start()
        copies.append(copy)
    mine = gathered[spec]
    mixed = dot(mine, mixer[pl.ds(pl.multiple_of(spec * width, width), width), :])
    for copy in copies:
        copy.wait()
    for d in range(1, groups):
        origin = lax.rem(spec + groups - d, groups)
        mixed = mixed + dot(
            gathered[origin], mixer[pl.ds(pl.multiple_of(origin * width, width), width), :]
        )
    state = mixed.astype(BF16)
    state_ref[...] = state

    top_to_low = onehot(same_species & (iota((width, width), 0) % layers == 0))
    spread_top = jnp.where(own_low, dot(state, top_to_low), 0.0).astype(BF16)
    digit_slot = onehot(iota((digits, slots), 0) == iota((digits, slots), 1) // RADIX)
    table = dot(digit_slot, spread_top).T.astype(BF16)
    for e in range(0, entries, block):
        high = recv_ref[species : species + 1, e : e + block].astype(jnp.int32)
        low = recv_ref[species + 1 : species + 2, e : e + block].astype(jnp.int32)
        high_hot = onehot(high == iota((digits, block), 0))
        low_hit = low == iota((RADIX, block), 0)
        found = dot(table, high_hot)
        for s in range(species):
            answer_ref[s : s + 1, e : e + block] = jnp.sum(
                jnp.where(low_hit, found[s * RADIX : (s + 1) * RADIX, :], 0.0), axis=0, keepdims=True
            )


def combine_kernel(capacity, returned_ref, part_ref, rank_ref, weight_ref, bottom_ref):
    per_cell, cells = part_ref.shape
    species = bottom_ref.shape[0]
    tiles = returned_ref.shape[1]
    totals = [jnp.zeros((1, cells), F32) for _ in range(species)]
    for r in range(per_cell):
        owner = onehot(part_ref[r : r + 1, :] == iota((tiles, cells), 0))
        place = rank_ref[r : r + 1, :].astype(jnp.int32) == iota((capacity, cells), 0)
        found = dot(returned_ref[...], owner)
        for s in range(species):
            picked = jnp.sum(
                jnp.where(place, found[s * capacity : (s + 1) * capacity, :], 0.0),
                axis=0,
                keepdims=True,
            )
            totals[s] = totals[s] + weight_ref[r : r + 1, :] * picked
    for s in range(species):
        bottom_ref[s : s + 1, :] = totals[s]


def whole():
    return pl.BlockSpec(memory_space=pltpu.VMEM)


def body(
    grad_columns,
    grad_flux,
    remap_part,
    remap_slot,
    remap_weight,
    col_count,
    neighbors,
    kappa,
    thickness,
    vertical,
    reaction,
):
    tiles, groups = lax.axis_size("tile"), lax.axis_size("spec")
    slots, width = grad_columns.shape
    species, layers = thickness.shape
    cells, per_cell = remap_part.shape
    capacity = 2 * cells * per_cell // tiles
    rim = slots // 8
    part_t, slot_t, weight_t = remap_part.T, remap_slot.T, remap_weight.T
    send, rank = pl.pallas_call(
        functools.partial(dispatch_kernel, tiles, capacity),
        out_shape=(
            jax.ShapeDtypeStruct((tiles, PLANES * capacity), BF16),
            jax.ShapeDtypeStruct((per_cell, cells), F32),
        ),
        in_specs=[whole()] * 4,
        out_specs=(whole(), whole()),
        compiler_params=pltpu.CompilerParams(vmem_limit_bytes=40 * 2**20),
        name="dispatch",
    )(part_t, slot_t, weight_t, grad_flux)
    recv = lax.all_to_all(send, "tile", split_axis=0, concat_axis=0, tiled=True)
    recv = recv.reshape(tiles, PLANES, capacity).transpose(1, 0, 2)
    recv = recv.reshape(PLANES, tiles * capacity).astype(F32)
    entries = tiles * capacity
    grad_state, answer = pl.pallas_call(
        functools.partial(column_kernel, tiles, groups),
        out_shape=(
            jax.ShapeDtypeStruct((slots, width), BF16),
            jax.ShapeDtypeStruct((species, entries), F32),
        ),
        in_specs=[whole(), whole(), pl.BlockSpec(memory_space=pltpu.SMEM)] + [whole()] * 5,
        out_specs=(whole(), whole()),
        scratch_shapes=[
            pltpu.VMEM((slots + 2 * rim, slots), BF16),
            pltpu.VMEM((slots, width), F32),
            pltpu.VMEM((width, width), BF16),
            pltpu.VMEM((groups * width, width), BF16),
            pltpu.VMEM((SUB, 2 * rim, width), BF16),
            pltpu.VMEM((SUB, 2 * rim, width), BF16),
            pltpu.VMEM((groups, slots, width), BF16),
            pltpu.SemaphoreType.DMA((SUB, 2)),
            pltpu.SemaphoreType.DMA((SUB, 2)),
            pltpu.SemaphoreType.DMA((groups - 1,)),
            pltpu.SemaphoreType.DMA((groups - 1,)),
        ],
        compiler_params=pltpu.CompilerParams(
            collective_id=0, has_side_effects=True, vmem_limit_bytes=48 * 2**20
        ),
        name="columns",
    )(
        recv,
        grad_columns,
        col_count.reshape(1, 1),
        neighbors.T,
        kappa.reshape(1, species),
        thickness,
        vertical.reshape(width, layers),
        reaction,
    )
    answer = answer.astype(BF16).reshape(species, tiles, capacity).transpose(1, 0, 2)
    answer = answer.reshape(tiles, species * capacity)
    returned = lax.all_to_all(answer, "tile", split_axis=0, concat_axis=0, tiled=True)
    grad_bottom = pl.pallas_call(
        functools.partial(combine_kernel, capacity),
        out_shape=jax.ShapeDtypeStruct((species, cells), F32),
        in_specs=[whole()] * 4,
        out_specs=whole(),
        compiler_params=pltpu.CompilerParams(vmem_limit_bytes=40 * 2**20),
        name="combine",
    )(returned.T, part_t, rank, weight_t)
    return (grad_state, grad_bottom)


def solution(mesh):
    placed = (
        P("tile", "spec"),
        P("spec", "tile"),
        P("tile", None),
        P("tile", None),
        P("tile", None),
        P("tile"),
        P("tile", None),
        P("spec"),
        P("spec", None),
        P("spec", None, None),
        P(None, "spec"),
    )
    return jax.shard_map(
        body,
        mesh=mesh,
        in_specs=placed,
        out_specs=(P("tile", "spec"), P("spec", "tile")),
        check_vma=False,
    )
```

time: 339 us -> 102 us (0.30); the launches traced: 333 us -> 101 us
  local copies, waits for them, and re-layouts: 92.6 us -> 8.19 us
  other arithmetic: 55.5 us -> 1.37 us
  waiting for transfers between devices: 70.3 us -> 23 us
  starting transfers between devices: 71.2 us -> 32 us
  Pallas kernels: 0 us -> 35 us
  matrix products: 28.2 us -> 0 us
  between operations: 15.5 us -> 1.48 us
    scatter-add x1 -> x0, other arithmetic: 44.8 us -> none  [body(): injected = jnp.zeros((col_max + 1, species), jnp.float32).at[slot_index]....]
    all_gather x1 -> x0, waiting for transfers between devices: 37.7 us -> none  [body(): piece = lax.all_gather(rounded, 'spec', axis=1, tiled=True)]
    gather x2 -> x0, local copies, waits for them, and re-layouts: 37 us -> none  [the longest x1 24 us: body(): answer = padded_top[slot_index].reshape(tiles, capacity, species)]
    pallas_call x0 -> x3, Pallas kernels: none -> 35 us  [the longest x1 31.1 us: body(): pl.pallas_call(functools.partial(column_kernel, tiles, groups), out_shape...]
    scatter x2 -> x0, local copies, waits for them, and re-layouts: 28.3 us -> none  [the longest x1 15.5 us: body(): send_slots = jnp.full((tiles * capacity, 1), col_max, jnp.int32).at[bucke...]
    dot_general x9 -> x0, matrix products: 28.2 us -> none  [the longest x4 25.4 us: body(): jnp.dot(count_matrix, spread, precision=lax.Precision.HIGHEST, preferred_...]
    ppermute x8 -> x0, starting transfers between devices: 22.3 us -> none  [shifted(): return lax.ppermute(block, axis, route)]
    all_to_all x3 -> x2, starting transfers between devices: 48.9 us -> 32 us  [the longest x1 18.4 us: body(): recv = lax.all_to_all(send, 'tile', split_axis=0, concat_axis=0, tiled=True)]
  transfers between devices with their start and end apart: 12 -> 2, of which waited for: 7 -> 2; matrix products, arithmetic and copies ran while one was open for 7% -> 0% of each run, Pallas kernels for 0% -> 0%
where the time goes in v1:
time: 102 us; the launch traced here: 101 us
  Pallas kernels  35 us (34%)
  starting transfers between devices  32 us (31%)
  waiting for transfers between devices  23 us (23%)
  local copies, waits for them, and re-layouts  8.19 us (8%)
  between operations  1.48 us (1%)
  other arithmetic  1.37 us (1%)
    pallas_call x1, Pallas kernels, body(): pl.pallas_call(functools.partial(column_kernel, tiles, groups), out_shape...  31.1 us
    all_to_all x1, starting transfers between devices, body(): recv = lax.all_to_all(send, 'tile', split_axis=0, concat_axis=0, tiled=True)  18.4 us
    all_to_all x1, starting transfers between devices, body(): lax.all_to_all(answer, 'tile', split_axis=0, concat_axis=0, tiled=True)  13.6 us
    all_to_all x1, waiting for transfers between devices, body(): lax.all_to_all(answer, 'tile', split_axis=0, concat_axis=0, tiled=True)  11.5 us
    all_to_all x1, waiting for transfers between devices, body(): recv = lax.all_to_all(send, 'tile', split_axis=0, concat_axis=0, tiled=True)  11.5 us
    unnamed x31, local copies, waits for them, and re-layouts  6.79 us
    pallas_call x1, Pallas kernels, body(): pl.pallas_call(functools.partial(dispatch_kernel, tiles, capacity), out_s...  2.19 us
  transfers between devices with their start and end apart: 2, of which 2 were waited for; matrix products, arithmetic and copies ran while one was open for 0% of the time, Pallas kernels for 0%

profile of v1, /device:TPU:1, one launch (start us, length us, event | category | flops | bytes accessed | tf_op | source)
XLA Modules:
  0.0 101.0 jit_solution(8415808219306098213)
XLA Ops:
  0.6 0.7 copy-done.1
  1.4 0.7 copy-done.3
  2.1 0.7 copy-done.7
  2.8 0.7 copy-done.8
  3.5 2.2 %dispatch.1 = (bf16[128,384]{1,0:T(8,128)(2,1)S(1)}, f32[4,1024]{1,0:T(4,128)S(1)}) custom-call(s32[4,1024]{1,0:T(4,128)S(1)} %bitcast.20, s32[4,1024]{1,0:T(4,128)S(1)} %bitcast.26, f32[4,1024]{1,0:T(4,128)S(1)} %bitcast.22, f32[4,1024]{1,0:T(4,128)S(1)} %copy-done.8), custom_call_target="tpu_custom_call" | custom-call | tf_op jit(solution)/shard_map/dispatch/pallas_call | solution.py:275
  5.7 0.5 broadcast
  6.2 0.7 reduce
  6.9 0.8 reshape.35
  7.7 18.4 %all-to-all-start = ((bf16[128,2,192]{2,1,0:T(2,128)(2,1)}), bf16[128,2,192]{2,1,0:T(2,128)(2,1)S(1)}, u32[]{:S(2)}, u32[]{:S(2)}) async-start(bf16[128,2,192]{2,1,0:T(2,128)(2,1)} %reshape.35), calls=%async_computation | async-start | bytes 262144 | tf_op jit(solution)/shard_map/all_to_all | solution.py:286
  26.9 11.5 %all-to-all-done = bf16[128,2,192]{2,1,0:T(2,128)(2,1)S(1)} async-done(((bf16[128,2,192]{2,1,0:T(2,128)(2,1)}), bf16[128,2,192]{2,1,0:T(2,128)(2,1)S(1)}, u32[]{:S(2)}, u32[]{:S(2)}) %all-to-all-start) | async-done | bytes 98336 | tf_op jit(solution)/shard_map/all_to_all | solution.py:286
  38.4 0.2 reshape.36
  38.5 0.2 copy.26
  38.7 0.2 copy.27
  39.0 0.1 reshape.33.recv_ref
  39.1 0.8 copy-done
  39.9 31.1 %columns.1 = (bf16[1024,128]{1,0:T(8,128)(2,1)S(1)}, f32[4,8192]{1,0:T(4,128)S(1)}) custom-call(f32[6,8192]{1,0:T(8,128)S(1)} %reshape.33.recv_ref, bf16[1024,128]{1,0:T(8,128)(2,1)S(1)} %copy-done, s32[1,1]{1,0:T(1,128)} %bitcast.17.count_ref, s32[4,1024]{1,0:T(4,128)S(1)} %bitcast.25, f32[1,4]{1,0:T(1,128)S(1)} %bitcast.27, f32[4,32]{1,0:T(4,128)S(1)} %copy-done.9, ...), custom_call_target="tpu_custom_call" | custom-call | tf_op jit(solution)/shard_map/columns/pallas_call | solution.py:290
  71.1 0.2 reshape.32
  71.4 0.7 reduce.1
  72.1 0.7 reshape.37
  72.8 13.6 %all-to-all-start.1 = ((bf16[128,2,128]{2,1,0:T(2,128)(2,1)}), bf16[128,2,128]{2,1,0:T(2,128)(2,1)S(1)}, u32[]{:S(2)}, u32[]{:S(2)}) async-start(bf16[128,2,128]{2,1,0:T(2,128)(2,1)} %reshape.37), calls=%async_computation.1 | async-start | bytes 131072 | tf_op jit(solution)/shard_map/all_to_all | solution.py:327
  86.4 11.5 %all-to-all-done.1 = bf16[128,2,128]{2,1,0:T(2,128)(2,1)S(1)} async-done(((bf16[128,2,128]{2,1,0:T(2,128)(2,1)}), bf16[128,2,128]{2,1,0:T(2,128)(2,1)S(1)}, u32[]{:S(2)}, u32[]{:S(2)}) %all-to-all-start.1) | async-done | bytes 65568 | tf_op jit(solution)/shard_map/all_to_all | solution.py:327
  98.1 0.6 copy-done.2
  98.7 1.6 %combine.1 = f32[4,1024]{1,0:T(4,128)} custom-call(bf16[256,128]{1,0:T(8,128)(2,1)S(1)} %bitcast.18, s32[4,1024]{1,0:T(4,128)S(1)} %bitcast.21, f32[4,1024]{1,0:T(4,128)S(1)} %get-tuple-element.9.rank_ref, f32[4,1024]{1,0:T(4,128)S(1)} %bitcast.23), custom_call_target="tpu_custom_call" | custom-call | tf_op jit(solution)/shard_map/combine/pallas_call | solution.py:328
  100.3 0.7 copy.36
  (25 shorter events, 0.6 us)
Async XLA Ops:
  0.6 0.7 copy-start.1
  1.4 0.7 copy-start.3
  2.1 0.7 copy-start.7
  2.8 0.7 copy-start.8
  7.7 30.7 %all-to-all-start = ((bf16[128,2,192]{2,1,0:T(2,128)(2,1)}), bf16[128,2,192]{2,1,0:T(2,128)(2,1)S(1)}, u32[]{:S(2)}, u32[]{:S(2)}) async-start(bf16[128,2,192]{2,1,0:T(2,128)(2,1)} %reshape.35), calls=%async_computation | async-start | bytes 262144 | tf_op jit(solution)/shard_map/all_to_all | solution.py:286
  26.1 0.7 copy-start.11
  38.9 1.0 copy-start
  38.9 0.9 copy-start.5
  38.9 0.9 copy-start.6
  39.1 0.8 copy-start.9
  39.1 0.8 copy-start.10
  72.8 25.1 %all-to-all-start.1 = ((bf16[128,2,128]{2,1,0:T(2,128)(2,1)}), bf16[128,2,128]{2,1,0:T(2,128)(2,1)S(1)}, u32[]{:S(2)}, u32[]{:S(2)}) async-start(bf16[128,2,128]{2,1,0:T(2,128)(2,1)} %reshape.37), calls=%async_computation.1 | async-start | bytes 131072 | tf_op jit(solution)/shard_map/all_to_all | solution.py:327
  98.0 0.7 copy-start.2
  98.0 0.7 copy-start.4

commit v2 on v1

v2 whole, which is shorter than its diff:
```python
import functools

import jax
import jax.numpy as jnp
from jax import lax
from jax.experimental import pallas as pl
from jax.experimental.pallas import tpu as pltpu
from jax.sharding import PartitionSpec as P

SUB = 4
F32 = jnp.float32
BF16 = jnp.bfloat16
MESH = pl.DeviceIdType.MESH
HIGH = lax.Precision.HIGHEST
NT = (((1,), (1,)), ((), ()))
RADIX = 32
ROW = 16


def dot(a, b):
    return jnp.dot(a, b, preferred_element_type=F32)


def iota(shape, dim):
    return lax.broadcasted_iota(jnp.int32, shape, dim)


def onehot(condition):
    return jnp.where(condition, 1.0, 0.0).astype(BF16)


def exchange(tile, spec, outer, source, stage, target, sems, between):
    mine, row = lax.rem(tile, ROW), tile // ROW
    first_send, first_recv, second_send, second_recv, local = sems
    keep = pltpu.make_async_copy(source.at[:, mine], stage.at[:, mine], local.at[0])
    keep.start()
    copies = []
    for d in range(1, ROW):
        other = lax.rem(mine + d, ROW)
        copy = pltpu.make_async_remote_copy(
            src_ref=source.at[:, other],
            dst_ref=stage.at[:, mine],
            send_sem=first_send.at[d - 1],
            recv_sem=first_recv.at[d - 1],
            device_id=(row * ROW + other, spec),
            device_id_type=MESH,
        )
        copy.start()
        copies.append(copy)
    between[0]()
    keep.wait()
    for copy in copies:
        copy.wait()
    keep = pltpu.make_async_copy(stage.at[row], target.at[row], local.at[1])
    keep.start()
    copies = []
    for d in range(1, outer):
        other = lax.rem(row + d, outer)
        copy = pltpu.make_async_remote_copy(
            src_ref=stage.at[other],
            dst_ref=target.at[row],
            send_sem=second_send.at[d - 1],
            recv_sem=second_recv.at[d - 1],
            device_id=(other * ROW + mine, spec),
            device_id_type=MESH,
        )
        copy.start()
        copies.append(copy)
    between[1]()
    keep.wait()
    for copy in copies:
        copy.wait()


def step_kernel(
    tiles,
    groups,
    part_hbm,
    slot_hbm,
    weight_hbm,
    flux_hbm,
    columns_hbm,
    neighbors_hbm,
    vertical_hbm,
    thickness_ref,
    count_ref,
    kappa_ref,
    reaction_ref,
    state_ref,
    bottom_ref,
    part_ref,
    slot_ref,
    weight_ref,
    flux_ref,
    columns_ref,
    neighbors_ref,
    vertical_ref,
    rank_ref,
    packed,
    names,
    adjoint,
    operator,
    mixer,
    send,
    stage,
    recv,
    answer,
    back,
    returned,
    halo_out,
    halo_in,
    gathered,
    tables,
    load_sem,
    halo_send,
    halo_recv,
    gather_send,
    gather_recv,
    table_send,
    table_recv,
    *sems,
):
    slots, width = columns_ref.shape
    species, layers = thickness_ref.shape
    per_cell, cells = part_ref.shape
    outer = tiles // ROW
    half = width // 2
    rim = slots // 8
    nbr_count = neighbors_ref.shape[0]
    tile, spec = lax.axis_index("tile"), lax.axis_index("spec")
    mine, row = lax.rem(tile, ROW), tile // ROW
    following = lax.rem(tile + 1, tiles)
    previous = lax.rem(tile + tiles - 1, tiles)
    peers = [lax.rem(spec + d, groups) for d in range(1, groups)]

    loads = []
    for k, (src, dst) in enumerate(
        (
            (part_hbm, part_ref),
            (slot_hbm, slot_ref),
            (weight_hbm, weight_ref),
            (flux_hbm, flux_ref),
            (neighbors_hbm, neighbors_ref),
            (columns_hbm, columns_ref),
            (vertical_hbm, vertical_ref),
        )
    ):
        load = pltpu.make_async_copy(src, dst, load_sem.at[k])
        load.start()
        loads.append(load)

    barrier = pltpu.get_barrier_semaphore()
    partners = [(other, spec) for other in (previous, following)]
    partners += [(tile, other) for other in peers]
    partners += [(row * ROW + lax.rem(mine + d, ROW), spec) for d in range(1, ROW)]
    partners += [(lax.rem(row + d, outer) * ROW + mine, spec) for d in range(1, outer)]
    for partner in partners:
        pl.semaphore_signal(barrier, inc=1, device_id=partner, device_id_type=MESH)

    for load in loads[:4]:
        load.wait()
    chunk = 256
    before = onehot(iota((chunk, chunk), 0) < iota((chunk, chunk), 1))
    carry = jnp.zeros((tiles, 1), F32)
    total = jnp.zeros((tiles, 4 * width), F32)
    for r in range(per_cell):
        hit = part_ref[r : r + 1, :] == iota((tiles, cells), 0)
        owner = jnp.where(hit, 1.0, 0.0)
        owner_b = owner.astype(BF16)
        for k in range(0, cells, chunk):
            piece = owner[:, k : k + chunk]
            earlier = dot(owner_b[:, k : k + chunk], before) + carry
            rank_ref[r : r + 1, k : k + chunk] = jnp.sum(piece * earlier, axis=0, keepdims=True)
            carry = carry + jnp.sum(piece, axis=1, keepdims=True)
        place = rank_ref[r : r + 1, :].astype(jnp.int32) == iota((half, cells), 0)
        slot = slot_ref[r : r + 1, :]
        weight = weight_ref[r : r + 1, :]
        rows = [weight * flux_ref[s : s + 1, :] for s in range(species)]
        rows.append((slot // RADIX).astype(F32))
        rows.append((slot % RADIX).astype(F32))
        pieces = [jnp.where(place, value, 0.0).astype(BF16) for value in rows]
        pieces = pieces[:5] + pieces[4:] + pieces[5:]
        wide = jnp.concatenate(pieces, axis=0)
        total = total + lax.dot_general(owner_b, wide, NT, preferred_element_type=F32)
    for k in range(4):
        packed[pl.ds(k, tiles, stride=4), :] = total[:, k * width : (k + 1) * width]
    for d in range(tiles):
        send[d // ROW, d % ROW] = packed[4 * d : 4 * d + 4, :].astype(BF16)

    step = 256

    def name(m):
        code = iota((step, slots), 0) + m
        count = jnp.zeros((step, slots), F32)
        for n in range(nbr_count):
            count = count + jnp.where(neighbors_ref[n : n + 1, :] == code, 1.0, 0.0)
        names[m : m + step, :] = count.astype(BF16)

    def under_first():
        loads[4].wait()
        for m in range(0, 3 * step, step):
            name(m)

    same_species = iota((width, width), 0) // layers == iota((width, width), 1) // layers

    def under_second():
        for m in range(3 * step, slots + 2 * rim, step):
            name(m)
        layer_to_lane = onehot(iota((layers, width), 0) == iota((layers, width), 1) % layers)
        for load in loads[5:]:
            load.wait()
        tall = dot(vertical_ref[...], layer_to_lane)
        operator[...] = jnp.where(same_species, tall, 0.0).astype(BF16)
        all_species = groups * species
        wide = groups * width
        row_species = onehot(iota((wide, all_species), 0) // layers == iota((wide, all_species), 1))
        lane_species = onehot(iota((species, width), 0) == iota((species, width), 1) // layers)
        by_row = lax.dot_general(row_species, reaction_ref[...], NT, preferred_element_type=F32)
        spread_out = dot(by_row.astype(BF16), lane_species)
        same_layer = iota((wide, width), 0) % layers == iota((wide, width), 1) % layers
        mixer[...] = jnp.where(same_layer, spread_out, 0.0).astype(BF16)

    pl.semaphore_wait(barrier, len(partners))
    exchange(
        tile, spec, outer, send, stage, recv, [s.at[0] for s in sems], (under_first, under_second)
    )

    lane = iota((1, width), 1)
    left = lane < half
    rate = jnp.zeros((1, width), F32)
    for s in range(species):
        rate = rate + jnp.where(lane // layers == s, kappa_ref[0:1, s : s + 1], 0.0)
    thick_rows = jnp.dot(
        thickness_ref[...],
        jnp.where(iota((layers, width), 0) == iota((layers, width), 1) % layers, 1.0, 0.0),
        precision=HIGH,
        preferred_element_type=F32,
    )
    thick = jnp.zeros((1, width), F32)
    for s in range(species):
        thick = thick + jnp.where(lane // layers == s, thick_rows[s : s + 1, :], 0.0)

    digits = slots // RADIX
    digit = iota((digits, width), 0)

    def inject(o, injected):
        highs, wides = [], []
        for i in range(ROW):
            x = recv[o, i].astype(F32)
            highs.append(onehot(x[2:3, :].astype(jnp.int32) == digit))
            low_hit = x[3:4, :].astype(jnp.int32) == digit
            values = []
            for s in range(species):
                value = jnp.where(left if s % 2 == 0 else ~left, x[s // 2 : s // 2 + 1, :], 0.0)
                values.append(jnp.where(low_hit, value, 0.0).astype(BF16))
            wides.append(jnp.concatenate(values, axis=0))
        return injected + lax.dot_general(
            jnp.concatenate(highs, axis=1),
            jnp.concatenate(wides, axis=1),
            NT,
            preferred_element_type=F32,
        )

    injected = lax.fori_loop(0, outer, inject, jnp.zeros((digits, width), F32))
    slot_digit = onehot(iota((slots, digits), 0) // RADIX == iota((slots, digits), 1))
    own_low = iota((slots, width), 0) % RADIX == iota((slots, width), 1) % RADIX
    block_ones = onehot(same_species)
    upper = injected.astype(BF16)
    lower = (injected - upper.astype(F32)).astype(BF16)
    added = jnp.zeros((slots, width), F32)
    for part in (upper, lower):
        chosen = jnp.where(own_low, dot(slot_digit, part), 0.0).astype(BF16)
        added = added + dot(chosen, block_ones)
    live = iota((slots, 1), 0) < count_ref[0, 0]
    adjoint[...] = jnp.where(live, columns_ref[...].astype(F32) + thick * added, 0.0)

    keep = 1.0 - nbr_count * rate
    for substep in range(SUB):
        spread = (rate * adjoint[...]).astype(BF16)
        outside = dot(names[slots : slots + 2 * rim, :], spread)
        halo_out[substep] = outside.astype(BF16)
        copies = []
        for side, other in enumerate((previous, following)):
            copy = pltpu.make_async_remote_copy(
                src_ref=halo_out.at[substep, pl.ds(side * rim, rim)],
                dst_ref=halo_in.at[substep, pl.ds((1 - side) * rim, rim)],
                send_sem=halo_send.at[substep, side],
                recv_sem=halo_recv.at[substep, side],
                device_id=(other, spec),
                device_id_type=MESH,
            )
            copy.start()
            copies.append(copy)
        inner = dot(names[0:slots, :], spread)
        bedload = keep * adjoint[...] + inner
        rest = bedload[2 * rim :, :].astype(BF16)
        rest = dot(rest, operator[...])
        for copy in copies:
            copy.wait()
        front = bedload[: 2 * rim, :] + halo_in[substep].astype(F32)
        front = dot(front.astype(BF16), operator[...])
        if substep < SUB - 1:
            adjoint[0 : 2 * rim, :] = front
            adjoint[2 * rim :, :] = rest
        else:
            gathered[spec, 0 : 2 * rim, :] = front.astype(BF16)
            gathered[spec, 2 * rim :, :] = rest.astype(BF16)

    own = gathered[spec]
    top_to_low = onehot(same_species & (iota((width, width), 0) % layers == 0))
    spread_top = jnp.where(own_low, dot(own, top_to_low), 0.0).astype(BF16)
    digit_slot = onehot(iota((digits, slots), 0) == iota((digits, slots), 1) // RADIX)
    tables[spec] = dot(digit_slot, spread_top).astype(BF16)

    def share(buffer, send_sem, recv_sem):
        copies = []
        for d, other in enumerate(peers):
            copy = pltpu.make_async_remote_copy(
                src_ref=buffer.at[spec],
                dst_ref=buffer.at[spec],
                send_sem=send_sem.at[d],
                recv_sem=recv_sem.at[d],
                device_id=(tile, other),
                device_id_type=MESH,
            )
            copy.start()
            copies.append(copy)
        return copies

    table_copies = share(tables, table_send, table_recv)
    gather_copies = share(gathered, gather_send, gather_recv)

    def mixer_of(origin):
        return mixer[pl.ds(pl.multiple_of(origin * width, width), width), :]

    for copy in table_copies:
        copy.wait()
    table = jnp.zeros((digits, width), F32)
    for g in range(groups):
        table = table + dot(tables[g], mixer[g * width : (g + 1) * width, :])
    table = table.T.astype(BF16)

    def reply(o, carried):
        highs, hits = [], []
        for i in range(ROW):
            x = recv[o, i].astype(F32)
            highs.append(onehot(x[2:3, :].astype(jnp.int32) == digit))
            hits.append(x[3:4, :].astype(jnp.int32) == digit)
        found = dot(table, jnp.concatenate(highs, axis=1))
        for i in range(ROW):
            lines = []
            for k in range(species // 2):
                even, odd = [
                    found[s * RADIX : (s + 1) * RADIX, i * width : (i + 1) * width]
                    for s in (2 * k, 2 * k + 1)
                ]
                picked = jnp.where(hits[i], jnp.where(left, even, odd), 0.0)
                lines.append(jnp.sum(picked, axis=0, keepdims=True))
            answer[o, i] = jnp.concatenate(lines, axis=0).astype(BF16)
        return carried

    lax.fori_loop(0, outer, reply, 0)

    def under_reply():
        pass

    def under_return():
        mixed = dot(own, mixer_of(spec))
        for copy in gather_copies:
            copy.wait()
        for d in range(1, groups):
            origin = lax.rem(spec + groups - d, groups)
            mixed = mixed + dot(gathered[origin], mixer_of(origin))
        state_ref[...] = mixed.astype(BF16)

    exchange(
        tile,
        spec,
        outer,
        answer,
        back,
        returned,
        [s.at[1] for s in sems],
        (under_reply, under_return),
    )
    for p in range(tiles):
        packed[2 * p : 2 * p + 2, :] = returned[p // ROW, p % ROW].astype(F32)
    by_place = jnp.concatenate(
        [packed[pl.ds(k, tiles, stride=2), :].T for k in range(species // 2)], axis=0
    ).astype(BF16)
    totals = [jnp.zeros((1, cells), F32) for _ in range(species)]
    for r in range(per_cell):
        owner = onehot(part_ref[r : r + 1, :] == iota((tiles, cells), 0))
        place = rank_ref[r : r + 1, :].astype(jnp.int32) == iota((half, cells), 0)
        found = dot(by_place, owner)
        for s in range(species):
            picked = jnp.where(place, found[s * half : (s + 1) * half, :], 0.0)
            picked = jnp.sum(picked, axis=0, keepdims=True)
            totals[s] = totals[s] + weight_ref[r : r + 1, :] * picked
    for s in range(species):
        bottom_ref[s : s + 1, :] = totals[s]


def whole():
    return pl.BlockSpec(memory_space=pltpu.VMEM)


def body(
    grad_columns,
    grad_flux,
    remap_part,
    remap_slot,
    remap_weight,
    col_count,
    neighbors,
    kappa,
    thickness,
    vertical,
    reaction,
):
    tiles, groups = lax.axis_size("tile"), lax.axis_size("spec")
    slots, width = grad_columns.shape
    species, layers = thickness.shape
    cells, per_cell = remap_part.shape
    rim = slots // 8
    outer = tiles // ROW
    digits = slots // RADIX
    nbr_count = neighbors.shape[1]
    dma = pltpu.SemaphoreType.DMA
    vmem = pltpu.VMEM
    grad_state, grad_bottom = pl.pallas_call(
        functools.partial(step_kernel, tiles, groups),
        out_shape=(
            jax.ShapeDtypeStruct((slots, width), BF16),
            jax.ShapeDtypeStruct((species, cells), F32),
        ),
        in_specs=[pl.BlockSpec(memory_space=pl.ANY)] * 7
        + [whole(), pl.BlockSpec(memory_space=pltpu.SMEM), whole(), whole()],
        out_specs=(whole(), whole()),
        scratch_shapes=[
            vmem((per_cell, cells), jnp.int32),
            vmem((per_cell, cells), jnp.int32),
            vmem((per_cell, cells), F32),
            vmem((species, cells), F32),
            vmem((slots, width), BF16),
            vmem((nbr_count, slots), jnp.int32),
            vmem((width, layers), BF16),
            vmem((per_cell, cells), F32),
            vmem((4 * tiles, width), F32),
            vmem((slots + 2 * rim, slots), BF16),
            vmem((slots, width), F32),
            vmem((width, width), BF16),
            vmem((groups * width, width), BF16),
            vmem((outer, ROW, 4, width), BF16),
            vmem((outer, ROW, 4, width), BF16),
            vmem((outer, ROW, 4, width), BF16),
            vmem((outer, ROW, 2, width), BF16),
            vmem((outer, ROW, 2, width), BF16),
            vmem((outer, ROW, 2, width), BF16),
            vmem((SUB, 2 * rim, width), BF16),
            vmem((SUB, 2 * rim, width), BF16),
            vmem((groups, slots, width), BF16),
            vmem((groups, digits, width), BF16),
            dma((7,)),
            dma((SUB, 2)),
            dma((SUB, 2)),
            dma((groups - 1,)),
            dma((groups - 1,)),
            dma((groups - 1,)),
            dma((groups - 1,)),
            dma((2, ROW - 1)),
            dma((2, ROW - 1)),
            dma((2, outer - 1)),
            dma((2, outer - 1)),
            dma((2, 2)),
        ],
        compiler_params=pltpu.CompilerParams(
            collective_id=0, has_side_effects=True, vmem_limit_bytes=56 * 2**20
        ),
        name="step",
    )(
        remap_part.T,
        remap_slot.T,
        remap_weight.T,
        grad_flux,
        grad_columns,
        neighbors.T,
        vertical.reshape(width, layers),
        thickness,
        col_count.reshape(1, 1),
        kappa.reshape(1, species),
        reaction.T,
    )
    return (grad_state, grad_bottom)


def solution(mesh):
    placed = (
        P("tile", "spec"),
        P("spec", "tile"),
        P("tile", None),
        P("tile", None),
        P("tile", None),
        P("tile"),
        P("tile", None),
        P("spec"),
        P("spec", None),
        P("spec", None, None),
        P(None, "spec"),
    )
    return jax.shard_map(
        body,
        mesh=mesh,
        in_specs=placed,
        out_specs=(P("tile", "spec"), P("spec", "tile")),
        check_vma=False,
    )
```

time: 102 us -> 69.2 us (0.68)
  starting transfers between devices: 32 us -> 0 us
  Pallas kernels: 35 us -> 64.5 us
  waiting for transfers between devices: 23 us -> 0 us
  local copies, waits for them, and re-layouts: 8.19 us -> 2.28 us
  other arithmetic: 1.37 us -> 0 us
    all_to_all x2 -> x0, starting transfers between devices: 32 us -> none  [the longest x1 18.4 us: body(): recv = lax.all_to_all(send, 'tile', split_axis=0, concat_axis=0, tiled=True)]
    pallas_call x3 -> x1, Pallas kernels: 35 us -> 64.5 us  [body(): pl.pallas_call(functools.partial(step_kernel, tiles, groups), out_shape=(...]
    all_to_all x2 -> x0, waiting for transfers between devices: 23 us -> none  [the longest x1 11.5 us: body(): lax.all_to_all(answer, 'tile', split_axis=0, concat_axis=0, tiled=True)]
    unnamed x31 -> x4, local copies, waits for them, and re-layouts: 6.79 us -> 2.28 us
    all_to_all x2 -> x0, other arithmetic: 1.33 us -> none  [the longest x1 0.67 us: body(): recv = lax.all_to_all(send, 'tile', split_axis=0, concat_axis=0, tiled=True)]
  transfers between devices with their start and end apart: 2 -> 0, of which waited for: 2 -> 0; matrix products, arithmetic and copies ran while one was open for 0% -> 0% of each run, Pallas kernels for 0% -> 0%
where the time goes in v2:
time: 69.2 us; the launch traced here: 68 us
  Pallas kernels  64.5 us (93%)
  local copies, waits for them, and re-layouts  2.28 us (3%)
  between operations  1.3 us (2%)
    pallas_call x1, Pallas kernels, body(): pl.pallas_call(functools.partial(step_kernel, tiles, groups), out_shape=(...  64.5 us
    unnamed x4, local copies, waits for them, and re-layouts  2.28 us

profile of v2, /device:TPU:1, one launch (start us, length us, event | category | flops | bytes accessed | tf_op | source)
XLA Modules:
  0.0 68.0 jit_solution(16170121881123866992)
XLA Ops:
  1.3 64.5 %step.1 = (bf16[1024,128]{1,0:T(8,128)(2,1)}, f32[4,1024]{1,0:T(4,128)}) custom-call(s32[4,1024]{1,0:T(4,128)} %bitcast.10, s32[4,1024]{1,0:T(4,128)} %bitcast.11, f32[4,1024]{1,0:T(4,128)} %bitcast.12, f32[4,1024]{1,0:T(4,128)} %flux_hbm.1, bf16[1024,128]{1,0:T(8,128)(2,1)} %columns_hbm.1, s32[4,1024]{1,0:T(4,128)} %bitcast.13, bf16[128,32]{1,0:T(8,128)(2,1)} %bitcast.9, ...), custom_call_target="tpu_custom_call" | custom-call | tf_op jit(solution)/shard_map/step/pallas_call | solution.py:431
  65.7 0.0 copy-start
  65.8 1.7 %copy.16 = bf16[1024,128]{1,0:T(8,128)(2,1)} copy(bf16[1024,128]{1,0:T(8,128)(2,1)} %get-tuple-element.4) | data formatting | bytes 524288
  67.4 0.0 copy-done
  67.4 0.6 copy.17
Async XLA Ops:
  65.7 1.7 %copy-start = (f32[4,1024]{1,0:T(4,128)S(1)}, f32[4,1024]{1,0:T(4,128)}, u32[]{:S(2)}) copy-start(f32[4,1024]{1,0:T(4,128)} %get-tuple-element.5) | copy-start | bytes 49156

commit v3 on v2

--- a/solution.py
+++ b/solution.py
@@ -82,10 +82,10 @@
     columns_hbm,
     neighbors_hbm,
     vertical_hbm,
-    thickness_ref,
-    count_ref,
-    kappa_ref,
-    reaction_ref,
+    thickness_hbm,
+    count_hbm,
+    kappa_hbm,
+    reaction_hbm,
     state_ref,
     bottom_ref,
     part_ref,
@@ -95,6 +95,10 @@
     columns_ref,
     neighbors_ref,
     vertical_ref,
+    thickness_ref,
+    count_ref,
+    kappa_ref,
+    reaction_ref,
     rank_ref,
     packed,
     names,
@@ -111,6 +115,9 @@
     halo_in,
     gathered,
     tables,
+    digit_hot,
+    rims,
+    beyond,
     load_sem,
     halo_send,
     halo_recv,
@@ -143,6 +150,10 @@
             (neighbors_hbm, neighbors_ref),
             (columns_hbm, columns_ref),
             (vertical_hbm, vertical_ref),
+            (thickness_hbm, thickness_ref),
+            (count_hbm, count_ref),
+            (kappa_hbm, kappa_ref),
+            (reaction_hbm, reaction_ref),
         )
     ):
         load = pltpu.make_async_copy(src, dst, load_sem.at[k])
@@ -254,14 +265,16 @@
                 value = jnp.where(left if s % 2 == 0 else ~left, x[s // 2 : s // 2 + 1, :], 0.0)
                 values.append(jnp.where(low_hit, value, 0.0).astype(BF16))
             wides.append(jnp.concatenate(values, axis=0))
+        high_hot = jnp.concatenate(highs, axis=1)
+        digit_hot[o] = high_hot
         return injected + lax.dot_general(
-            jnp.concatenate(highs, axis=1),
             jnp.concatenate(wides, axis=1),
+            high_hot,
             NT,
             preferred_element_type=F32,
         )
 
-    injected = lax.fori_loop(0, outer, inject, jnp.zeros((digits, width), F32))
+    injected = lax.fori_loop(0, outer, inject, jnp.zeros((width, digits), F32)).T
     slot_digit = onehot(iota((slots, digits), 0) // RADIX == iota((slots, digits), 1))
     own_low = iota((slots, width), 0) % RADIX == iota((slots, width), 1) % RADIX
     block_ones = onehot(same_species)
@@ -271,13 +284,13 @@
     for part in (upper, lower):
         chosen = jnp.where(own_low, dot(slot_digit, part), 0.0).astype(BF16)
         added = added + dot(chosen, block_ones)
-    live = iota((slots, 1), 0) < count_ref[0, 0]
+    live = iota((slots, 1), 0) < count_ref[...]
     adjoint[...] = jnp.where(live, columns_ref[...].astype(F32) + thick * added, 0.0)
 
     keep = 1.0 - nbr_count * rate
-    for substep in range(SUB):
-        spread = (rate * adjoint[...]).astype(BF16)
-        outside = dot(names[slots : slots + 2 * rim, :], spread)
+    near = 2 * rim
+
+    def launch(substep, outside):
         halo_out[substep] = outside.astype(BF16)
         copies = []
         for side, other in enumerate((previous, following)):
@@ -291,20 +304,33 @@
             )
             copy.start()
             copies.append(copy)
-        inner = dot(names[0:slots, :], spread)
-        bedload = keep * adjoint[...] + inner
-        rest = bedload[2 * rim :, :].astype(BF16)
-        rest = dot(rest, operator[...])
+        return copies
+
+    spread = (rate * adjoint[...]).astype(BF16)
+    copies = launch(0, dot(names[slots:, :], spread))
+    adjoint[...] = keep * adjoint[...] + dot(names[0:slots, near:], spread[near:, :])
+    spread_front = spread[0:near, :]
+    for substep in range(SUB):
+        bed = adjoint[near:, :] + dot(names[near:slots, 0:near], spread_front)
+        rest = dot(bed.astype(BF16), operator[...])
+        rims[...] = adjoint[0:near, :] + dot(names[0:near, 0:near], spread_front)
+        if substep < SUB - 1:
+            spread_rest = (rate * rest).astype(BF16)
+            beyond[...] = dot(names[slots:, near:], spread_rest)
+            adjoint[near:, :] = keep * rest + dot(names[near:slots, near:], spread_rest)
+            adjoint[0:near, :] = dot(names[0:near, near:], spread_rest)
+        else:
+            gathered[spec, near:, :] = rest.astype(BF16)
         for copy in copies:
             copy.wait()
-        front = bedload[: 2 * rim, :] + halo_in[substep].astype(F32)
+        front = rims[...] + halo_in[substep].astype(F32)
         front = dot(front.astype(BF16), operator[...])
         if substep < SUB - 1:
-            adjoint[0 : 2 * rim, :] = front
-            adjoint[2 * rim :, :] = rest
+            spread_front = (rate * front).astype(BF16)
+            copies = launch(substep + 1, beyond[...] + dot(names[slots:, 0:near], spread_front))
+            adjoint[0:near, :] = adjoint[0:near, :] + keep * front
         else:
-            gathered[spec, 0 : 2 * rim, :] = front.astype(BF16)
-            gathered[spec, 2 * rim :, :] = rest.astype(BF16)
+            gathered[spec, 0:near, :] = front.astype(BF16)
 
     own = gathered[spec]
     top_to_low = onehot(same_species & (iota((width, width), 0) % layers == 0))
@@ -328,7 +354,26 @@
         return copies
 
     table_copies = share(tables, table_send, table_recv)
-    gather_copies = share(gathered, gather_send, gather_recv)
+
+    right, left_peer = lax.rem(spec + 1, groups), lax.rem(spec + groups - 1, groups)
+    middle = slots // 2
+
+    def pass_on(origin, start, other, index):
+        view = gathered.at[origin, pl.ds(start, middle)]
+        copy = pltpu.make_async_remote_copy(
+            src_ref=view,
+            dst_ref=view,
+            send_sem=gather_send.at[index],
+            recv_sem=gather_recv.at[index],
+            device_id=(tile, other),
+            device_id_type=MESH,
+        )
+        copy.start()
+        return copy
+
+    to_right = pass_on(spec, 0, right, 0)
+    to_left = pass_on(spec, middle, left_peer, 1)
+    gather_copies = [pass_on(spec, middle, right, 2), pass_on(spec, 0, left_peer, 3)]
 
     def mixer_of(origin):
         return mixer[pl.ds(pl.multiple_of(origin * width, width), width), :]
@@ -341,12 +386,11 @@
     table = table.T.astype(BF16)
 
     def reply(o, carried):
-        highs, hits = [], []
+        hits = []
         for i in range(ROW):
             x = recv[o, i].astype(F32)
-            highs.append(onehot(x[2:3, :].astype(jnp.int32) == digit))
             hits.append(x[3:4, :].astype(jnp.int32) == digit)
-        found = dot(table, jnp.concatenate(highs, axis=1))
+        found = dot(table, digit_hot[o])
         for i in range(ROW):
             lines = []
             for k in range(species // 2):
@@ -362,7 +406,10 @@
     lax.fori_loop(0, outer, reply, 0)
 
     def under_reply():
-        pass
+        to_right.wait()
+        to_left.wait()
+        gather_copies.append(pass_on(left_peer, 0, right, 4))
+        gather_copies.append(pass_on(right, middle, left_peer, 5))
 
     def under_return():
         mixed = dot(own, mixer_of(spec))
@@ -434,8 +481,7 @@
             jax.ShapeDtypeStruct((slots, width), BF16),
             jax.ShapeDtypeStruct((species, cells), F32),
         ),
-        in_specs=[pl.BlockSpec(memory_space=pl.ANY)] * 7
-        + [whole(), pl.BlockSpec(memory_space=pltpu.SMEM), whole(), whole()],
+        in_specs=[pl.BlockSpec(memory_space=pltpu.HBM)] * 11,
         out_specs=(whole(), whole()),
         scratch_shapes=[
             vmem((per_cell, cells), jnp.int32),
@@ -445,6 +491,10 @@
             vmem((slots, width), BF16),
             vmem((nbr_count, slots), jnp.int32),
             vmem((width, layers), BF16),
+            vmem((species, layers), F32),
+            vmem((1, 1), jnp.int32),
+            vmem((1, species), F32),
+            vmem((species, groups * species), BF16),
             vmem((per_cell, cells), F32),
             vmem((4 * tiles, width), F32),
             vmem((slots + 2 * rim, slots), BF16),
@@ -461,11 +511,14 @@
             vmem((SUB, 2 * rim, width), BF16),
             vmem((groups, slots, width), BF16),
             vmem((groups, digits, width), BF16),
-            dma((7,)),
+            vmem((outer, digits, ROW * width), BF16),
+            vmem((2 * rim, width), F32),
+            vmem((2 * rim, width), F32),
+            dma((11,)),
             dma((SUB, 2)),
             dma((SUB, 2)),
-            dma((groups - 1,)),
-            dma((groups - 1,)),
+            dma((6,)),
+            dma((6,)),
             dma((groups - 1,)),
             dma((groups - 1,)),
             dma((2, ROW - 1)),
@@ -475,7 +528,7 @@
             dma((2, 2)),
         ],
         compiler_params=pltpu.CompilerParams(
-            collective_id=0, has_side_effects=True, vmem_limit_bytes=56 * 2**20
+            collective_id=0, has_side_effects=True, vmem_limit_bytes=60 * 2**20
         ),
         name="step",
     )(

time: 69.2 us -> 67.6 us (0.977); the launches traced: 68 us -> 67.2 us
  Pallas kernels: 64.5 us -> 63.7 us
    pallas_call x1, Pallas kernels: 64.5 us -> 63.7 us  [body(): pl.pallas_call(functools.partial(step_kernel, tiles, groups), out_shape=(...]
where the time goes in v3:
time: 67.6 us; the launch traced here: 67.2 us
  Pallas kernels  63.7 us (94%)
  local copies, waits for them, and re-layouts  2.28 us (3%)
  between operations  1.3 us (2%)
    pallas_call x1, Pallas kernels, body(): pl.pallas_call(functools.partial(step_kernel, tiles, groups), out_shape=(...  63.7 us
    unnamed x4, local copies, waits for them, and re-layouts  2.28 us

profile of v3, /device:TPU:1, one launch (start us, length us, event | category | flops | bytes accessed | tf_op | source)
XLA Modules:
  0.0 67.2 jit_solution(5633775667975847773)
XLA Ops:
  1.3 63.7 %step.1 = (bf16[1024,128]{1,0:T(8,128)(2,1)}, f32[4,1024]{1,0:T(4,128)}) custom-call(s32[4,1024]{1,0:T(4,128)} %bitcast.10, s32[4,1024]{1,0:T(4,128)} %bitcast.11, f32[4,1024]{1,0:T(4,128)} %bitcast.12, f32[4,1024]{1,0:T(4,128)} %flux_hbm.1, bf16[1024,128]{1,0:T(8,128)(2,1)} %columns_hbm.1, s32[4,1024]{1,0:T(4,128)} %bitcast.13, bf16[128,32]{1,0:T(8,128)(2,1)} %bitcast.9, ...), custom_call_target="tpu_custom_call" | custom-call | tf_op jit(solution)/shard_map/step/pallas_call | solution.py:478
  64.9 0.0 copy-start
  65.0 1.7 %copy.16 = bf16[1024,128]{1,0:T(8,128)(2,1)} copy(bf16[1024,128]{1,0:T(8,128)(2,1)} %get-tuple-element.4) | data formatting | bytes 524288
  66.6 0.0 copy-done
  66.6 0.6 copy.17
Async XLA Ops:
  64.9 1.7 %copy-start = (f32[4,1024]{1,0:T(4,128)S(1)}, f32[4,1024]{1,0:T(4,128)}, u32[]{:S(2)}) copy-start(f32[4,1024]{1,0:T(4,128)} %get-tuple-element.5) | copy-start | bytes 49156

commit v4 on v3

--- a/solution.py
+++ b/solution.py
@@ -29,13 +29,22 @@
     return jnp.where(condition, 1.0, 0.0).astype(BF16)
 
 
+def farthest_first(count):
+    return sorted(range(1, count), key=lambda d: -min(d, count - d))
+
+
+def swap_halves(x):
+    half = x.shape[1] // 2
+    return jnp.concatenate([x[:, half:], x[:, :half]], axis=1)
+
+
 def exchange(tile, spec, outer, source, stage, target, sems, between):
     mine, row = lax.rem(tile, ROW), tile // ROW
     first_send, first_recv, second_send, second_recv, local = sems
     keep = pltpu.make_async_copy(source.at[:, mine], stage.at[:, mine], local.at[0])
     keep.start()
     copies = []
-    for d in range(1, ROW):
+    for d in farthest_first(ROW):
         other = lax.rem(mine + d, ROW)
         copy = pltpu.make_async_remote_copy(
             src_ref=source.at[:, other],
@@ -54,7 +63,7 @@
     keep = pltpu.make_async_copy(stage.at[row], target.at[row], local.at[1])
     keep.start()
     copies = []
-    for d in range(1, outer):
+    for d in farthest_first(outer):
         other = lax.rem(row + d, outer)
         copy = pltpu.make_async_remote_copy(
             src_ref=stage.at[other],
@@ -256,13 +265,16 @@
 
     def inject(o, injected):
         highs, wides = [], []
-        for i in range(ROW):
-            x = recv[o, i].astype(F32)
-            highs.append(onehot(x[2:3, :].astype(jnp.int32) == digit))
-            low_hit = x[3:4, :].astype(jnp.int32) == digit
+        for i in range(0, ROW, 2):
+            one, two = recv[o, i].astype(F32), recv[o, i + 1].astype(F32)
+            slots_of = jnp.where(left, one, two)
+            evens = jnp.where(left, one, swap_halves(two))
+            odds = jnp.where(left, swap_halves(one), two)
+            highs.append(onehot(slots_of[2:3, :].astype(jnp.int32) == digit))
+            low_hit = slots_of[3:4, :].astype(jnp.int32) == digit
             values = []
             for s in range(species):
-                value = jnp.where(left if s % 2 == 0 else ~left, x[s // 2 : s // 2 + 1, :], 0.0)
+                value = (evens if s % 2 == 0 else odds)[s // 2 : s // 2 + 1, :]
                 values.append(jnp.where(low_hit, value, 0.0).astype(BF16))
             wides.append(jnp.concatenate(values, axis=0))
         high_hot = jnp.concatenate(highs, axis=1)
@@ -386,21 +398,18 @@
     table = table.T.astype(BF16)
 
     def reply(o, carried):
-        hits = []
-        for i in range(ROW):
-            x = recv[o, i].astype(F32)
-            hits.append(x[3:4, :].astype(jnp.int32) == digit)
         found = dot(table, digit_hot[o])
-        for i in range(ROW):
+        for i in range(0, ROW, 2):
+            one, two = recv[o, i].astype(F32), recv[o, i + 1].astype(F32)
+            low_hit = jnp.where(left, one, two)[3:4, :].astype(jnp.int32) == digit
             lines = []
-            for k in range(species // 2):
-                even, odd = [
-                    found[s * RADIX : (s + 1) * RADIX, i * width : (i + 1) * width]
-                    for s in (2 * k, 2 * k + 1)
-                ]
-                picked = jnp.where(hits[i], jnp.where(left, even, odd), 0.0)
-                lines.append(jnp.sum(picked, axis=0, keepdims=True))
-            answer[o, i] = jnp.concatenate(lines, axis=0).astype(BF16)
+            for s in range(species):
+                block = found[s * RADIX : (s + 1) * RADIX, i // 2 * width : (i // 2 + 1) * width]
+                lines.append(jnp.sum(jnp.where(low_hit, block, 0.0), axis=0, keepdims=True))
+            evens = jnp.concatenate(lines[0::2], axis=0)
+            odds = jnp.concatenate(lines[1::2], axis=0)
+            answer[o, i] = jnp.where(left, evens, swap_halves(odds)).astype(BF16)
+            answer[o, i + 1] = jnp.where(left, swap_halves(evens), odds).astype(BF16)
         return carried
 
     lax.fori_loop(0, outer, reply, 0)
@@ -511,7 +520,7 @@
             vmem((SUB, 2 * rim, width), BF16),
             vmem((groups, slots, width), BF16),
             vmem((groups, digits, width), BF16),
-            vmem((outer, digits, ROW * width), BF16),
+            vmem((outer, digits, ROW // 2 * width), BF16),
             vmem((2 * rim, width), F32),
             vmem((2 * rim, width), F32),
             dma((11,)),

time: 67.6 us -> 66.3 us (0.981)
  Pallas kernels: 63.7 us -> 62.3 us
    pallas_call x1, Pallas kernels: 63.7 us -> 62.3 us  [body(): pl.pallas_call(functools.partial(step_kernel, tiles, groups), out_shape=(...]
where the time goes in v4:
time: 66.3 us; the launch traced here: 65.9 us
  Pallas kernels  62.3 us (94%)
  local copies, waits for them, and re-layouts  2.28 us (3%)
  between operations  1.3 us (2%)
    pallas_call x1, Pallas kernels, body(): pl.pallas_call(functools.partial(step_kernel, tiles, groups), out_shape=(...  62.3 us
    unnamed x4, local copies, waits for them, and re-layouts  2.28 us

profile of v4, /device:TPU:1, one launch (start us, length us, event | category | flops | bytes accessed | tf_op | source)
XLA Modules:
  0.0 65.9 jit_solution(17937191179837832783)
XLA Ops:
  1.3 62.3 %step.1 = (bf16[1024,128]{1,0:T(8,128)(2,1)}, f32[4,1024]{1,0:T(4,128)}) custom-call(s32[4,1024]{1,0:T(4,128)} %bitcast.10, s32[4,1024]{1,0:T(4,128)} %bitcast.11, f32[4,1024]{1,0:T(4,128)} %bitcast.12, f32[4,1024]{1,0:T(4,128)} %flux_hbm.1, bf16[1024,128]{1,0:T(8,128)(2,1)} %columns_hbm.1, s32[4,1024]{1,0:T(4,128)} %bitcast.13, bf16[128,32]{1,0:T(8,128)(2,1)} %bitcast.9, ...), custom_call_target="tpu_custom_call" | custom-call | tf_op jit(solution)/shard_map/step/pallas_call | solution.py:487
  63.6 0.0 copy-start
  63.6 1.7 %copy.16 = bf16[1024,128]{1,0:T(8,128)(2,1)} copy(bf16[1024,128]{1,0:T(8,128)(2,1)} %get-tuple-element.4) | data formatting | bytes 524288
  65.3 0.0 copy-done
  65.3 0.6 copy.17
Async XLA Ops:
  63.6 1.7 %copy-start = (f32[4,1024]{1,0:T(4,128)S(1)}, f32[4,1024]{1,0:T(4,128)}, u32[]{:S(2)}) copy-start(f32[4,1024]{1,0:T(4,128)} %get-tuple-element.5) | copy-start | bytes 49156

commit v5 on v4

--- a/solution.py
+++ b/solution.py
@@ -487,8 +487,8 @@
     grad_state, grad_bottom = pl.pallas_call(
         functools.partial(step_kernel, tiles, groups),
         out_shape=(
-            jax.ShapeDtypeStruct((slots, width), BF16),
-            jax.ShapeDtypeStruct((species, cells), F32),
+            vmem((slots, width), BF16),
+            vmem((species, cells), F32),
         ),
         in_specs=[pl.BlockSpec(memory_space=pltpu.HBM)] * 11,
         out_specs=(whole(), whole()),

time: 66.3 us -> 64.7 us (0.976)
  local copies, waits for them, and re-layouts: 2.28 us -> 1.31 us
    unnamed x4 -> x2, local copies, waits for them, and re-layouts: 2.28 us -> 1.31 us
where the time goes in v5:
time: 64.7 us; the launch traced here: 64.3 us
  Pallas kernels  61.7 us (95%)
  local copies, waits for them, and re-layouts  1.31 us (2%)
  between operations  1.29 us (2%)
    pallas_call x1, Pallas kernels, body(): pl.pallas_call(functools.partial(step_kernel, tiles, groups), out_shape=(...  61.7 us
    unnamed x2, local copies, waits for them, and re-layouts  1.31 us

profile of v5, /device:TPU:1, one launch (start us, length us, event | category | flops | bytes accessed | tf_op | source)
XLA Modules:
  0.0 64.3 jit_solution(17008057905124734236)
XLA Ops:
  1.3 61.7 %step.1 = (bf16[1024,128]{1,0:T(8,128)(2,1)S(1)}, f32[4,1024]{1,0:T(4,128)S(1)}) custom-call(s32[4,1024]{1,0:T(4,128)} %bitcast.10, s32[4,1024]{1,0:T(4,128)} %bitcast.11, f32[4,1024]{1,0:T(4,128)} %bitcast.12, f32[4,1024]{1,0:T(4,128)} %flux_hbm.1, bf16[1024,128]{1,0:T(8,128)(2,1)} %columns_hbm.1, s32[4,1024]{1,0:T(4,128)} %bitcast.13, ...), custom_call_target="tpu_custom_call" | custom-call | tf_op jit(solution)/shard_map/step/pallas_call | solution.py:487
  63.0 0.7 %copy.15 = bf16[1024,128]{1,0:T(8,128)(2,1)} copy(bf16[1024,128]{1,0:T(8,128)(2,1)S(1)} %get-tuple-element.2) | data formatting | bytes 524288
  63.7 0.6 copy.16
